TPU v7x, 32 devices: a whole 2x2x4 slice. The times are simulated.
32 devices in a mesh: section: 4 (over z), tile: 8 (over y, x, core).
Axes of the slice: x: 2, y: 2, z: 4, core: 2. Of those that a mesh axis runs over, the one named last changes fastest.
Arguments:
- raw_echo: bfloat16 [2, 2048, 8192], P(None, 'tile', 'section'), may hold values from -6 to 6
- footprint: int32 [4, 8, 8], P('section', 'tile'), may hold values from 0 to 255, as said below
- window_start: int32 [4, 256], P('section', 'tile'), may hold values from 0 to 2047
Outputs:
- image: bfloat16 [4, 8, 1024, 2048], P('section', 'tile')
Inputs may be any that keep to these rules, and one draw needn't show every extreme that they name: `footprint`: each list names 8 different pulse blocks; at most 2 of them lie among the 32 blocks k * 32 to (k + 1) * 32 - 1 of one index k of tile, and in every list some index supplies exactly 2.
All inputs are finite; a program needn't handle non-finite values.
Results may differ from a plain program's by a relative error of at most 0.0071.
Values may be sent and summed in bfloat16 or wider, within the bound.
No kernel may reach another device: no remote copies, remote signals or barrier semaphores. Data moves between devices by JAX's collectives and lax.ppermute only.
A program may use at most 128 MiB of HBM per device.

v0:
```python
import math
import jax
import jax.numpy as jnp
from jax import lax
from jax.sharding import PartitionSpec as P

KC = 128
WIN = 256
PR = 1024
PC = 1024
NP = 8


def passed_along(value, axis, by):
    devices = lax.axis_size(axis)
    pairs = [(i, i + by) for i in range(devices) if 0 <= i + by < devices]
    return lax.ppermute(value, axis, pairs)


def chirp_table(length):
    row_index = lax.broadcasted_iota(jnp.int32, (2 * length, length), 0)
    col_index = lax.broadcasted_iota(jnp.int32, (2 * length, length), 1)
    lag_count = row_index - col_index
    inside = (lag_count >= 0) & (lag_count < length)
    lag_safe = jnp.where(inside, lag_count, 0)
    turn_count = (lag_safe * lag_safe % (2 * length)).astype(jnp.float32)
    phase_angle = turn_count * jnp.float32(math.pi / length)
    scaling = jnp.float32(1.0 / math.sqrt(length))
    real_part = jnp.where(inside, jnp.cos(phase_angle) * scaling, jnp.float32(0.0))
    imag_part = jnp.where(inside, jnp.sin(phase_angle) * scaling, jnp.float32(0.0))
    return (real_part.astype(jnp.bfloat16), imag_part.astype(jnp.bfloat16))


def compress(raw_part, length, keep):
    real_tab, imag_tab = chirp_table(length)
    pulses = raw_part.shape[1]
    blocks = keep // length
    pieces = raw_part.reshape(2, pulses, blocks + 1, length)
    paired = jnp.concatenate([pieces[:, :, :-1], pieces[:, :, 1:]], axis=3).reshape(
        2, pulses * blocks, 2 * length
    )
    real_in = paired[0]
    imag_in = paired[1]
    out_real = jnp.dot(real_in, real_tab, preferred_element_type=jnp.float32) + jnp.dot(
        imag_in, imag_tab, preferred_element_type=jnp.float32
    )
    out_imag = jnp.dot(imag_in, real_tab, preferred_element_type=jnp.float32) - jnp.dot(
        real_in, imag_tab, preferred_element_type=jnp.float32
    )
    stacked = jnp.stack([out_real, out_imag]).reshape(2, pulses, keep)
    return stacked.astype(jnp.bfloat16)


def interp_table(pixel_rows, window_bins):
    upsample = pixel_rows // window_bins
    row_index = lax.broadcasted_iota(jnp.float32, (pixel_rows, window_bins), 0)
    bin_index = lax.broadcasted_iota(jnp.float32, (pixel_rows, window_bins), 1)
    centre = (row_index + 0.5) / upsample - 0.5
    offset = bin_index - centre
    tapering = jnp.cos(offset * (math.pi / 8.0)) ** 2
    kernel = jnp.where(jnp.abs(offset) < 4.0, jnp.sinc(offset) * tapering, 0.0)
    return kernel.astype(jnp.bfloat16)


def tile_image(chosen, block_ids, row_pos, col_pos, interp, pixel_cols):
    entries = chosen.shape[0]
    per_block = chosen.shape[1]
    window_bins = chosen.shape[3]
    merged = chosen.reshape(entries * per_block, 2 * window_bins)
    pulse_ids = (
        block_ids[:, None] * per_block + jnp.arange(per_block, dtype=jnp.int32)[None, :]
    ).reshape(-1)
    columns = col_pos * pixel_cols + jnp.arange(pixel_cols, dtype=jnp.int32) + 1 + 7 * row_pos
    scrambled = columns * 40503 % 65521
    residue = pulse_ids[:, None] * scrambled[None, :] % 65521
    phase_angle = residue.astype(jnp.float32) * jnp.float32(2.0 * math.pi / 65521.0)
    steer_real = jnp.cos(phase_angle).astype(jnp.bfloat16)
    steer_imag = jnp.sin(phase_angle).astype(jnp.bfloat16)
    contract = (((0,), (0,)), ((), ()))
    with_real = lax.dot_general(merged, steer_real, contract, preferred_element_type=jnp.float32)
    with_imag = lax.dot_general(merged, steer_imag, contract, preferred_element_type=jnp.float32)
    scaling = jnp.float32(1.0 / math.sqrt(entries * per_block))
    focus_real = (with_real[:window_bins] - with_imag[window_bins:]) * scaling
    focus_imag = (with_imag[:window_bins] + with_real[window_bins:]) * scaling
    focused = jnp.concatenate([focus_real, focus_imag], axis=1).astype(jnp.bfloat16)
    return jnp.dot(interp, focused, preferred_element_type=jnp.float32).astype(jnp.bfloat16)


def cut_windows(extended, starts, per_block):
    pulses = extended.shape[1]
    span_bins = extended.shape[2]
    grouped = jnp.transpose(
        extended.reshape(2, pulses // per_block, per_block, span_bins), (1, 2, 0, 3)
    )

    def one_block(block_data, start):
        return lax.dynamic_slice_in_dim(block_data, start, WIN, 2)

    return jax.vmap(one_block)(grouped, starts)


def local(raw_echo, footprint, window_start):
    bin_count = raw_echo.shape[2]
    next_rim = passed_along(raw_echo[:, :, :KC], "section", -1)
    own_part = compress(jnp.concatenate([raw_echo, next_rim], axis=2), KC, bin_count)
    next_bins = passed_along(own_part[:, :, :WIN], "section", -1)
    extended = jnp.concatenate([own_part, next_bins], axis=2)
    windows = cut_windows(extended, window_start[0], NP)
    my_list = footprint[0, 0]
    tile_pos = lax.axis_index("tile")
    row_pos = lax.axis_index("section")
    all_blocks = lax.all_gather(windows, "tile", axis=0, tiled=True)
    chosen = jnp.take(all_blocks, my_list, axis=0)
    interp = interp_table(PR, WIN)
    image = tile_image(chosen, my_list, row_pos, tile_pos, interp, PC)
    return image[None, None]


def solution(mesh):
    in_specs = (P(None, "tile", "section"), P("section", "tile", None), P("section", "tile"))
    out_specs = P("section", "tile", None, None)
    return jax.shard_map(local, mesh=mesh, in_specs=in_specs, out_specs=out_specs, check_vma=False)
```

profile of v0, /device:TPU:0, one launch (start us, length us, event | category | flops | bytes accessed | tf_op | source)
XLA Modules:
  0.0 181.1 jit_solution(12100500757804425028)
XLA Ops:
  6.5 0.0 all-gather.2.cloned.1.call-start
  6.5 2.8 %copy.15 = bf16[2,256,2048]{1,2,0:T(8,128)(2,1)S(1)} copy(bf16[2,256,2048]{2,1,0:T(8,128)(2,1)} %param.3) | data formatting | bytes 4194304 | tf_op args[0]
  9.4 1.3 collective-permute-start
  10.7 7.1 %collective-permute-done = bf16[2,256,128]{1,2,0:T(8,128)(2,1)S(1)} collective-permute-done((bf16[2,256,128]{1,2,0:T(8,128)(2,1)S(1)}, bf16[2,256,128]{1,2,0:T(8,128)(2,1)S(1)}, u32[]{:S(2)}, u32[]{:S(2)}) %collective-permute-start) | collective-permute-done | bytes 131104 | tf_op jit(solution)/shard_map/ppermute | solution.py:17
  17.8 0.1 pad_maximum_fusion
  18.0 0.5 fusion.123
  18.5 2.3 %pad_maximum_fusion.1 = (bf16[1,256,16,256]{1,3,2,0:T(8,128)(2,1)}, bf16[1,256,16,256]{1,3,2,0:T(8,128)(2,1)}) fusion(bf16[2,256,16,128]{1,3,2,0:T(8,128)(2,1)S(1)} %get-tuple-element.9, bf16[2,256,16,128]{1,3,2,0:T(8,128)(2,1)S(1)} %get-tuple-element.10), kind=kLoop, calls=%fused_computation.12 | loop fusion | flops 8388608 | bytes 8388608 | tf_op jit(solution)/shard_map/concatenate | solution.py:39
  20.8 3.3 %copy.17 = bf16[1,256,16,256]{3,2,1,0:T(8,128)(2,1)S(1)} copy(bf16[1,256,16,256]{1,3,2,0:T(8,128)(2,1)} %get-tuple-element.7) | data formatting | bytes 4194304 | tf_op jit(solution)/shard_map/slice | solution.py:43
  24.1 2.5 %fusion.63 = f32[4096,128]{1,0:T(8,128)} fusion(bf16[4096,256]{1,0:T(8,128)(2,1)S(1)} %bitcast.27), kind=kOutput, calls=%fused_computation.95 | convolution fusion | flops 269156352 | bytes 4194304 | tf_op jit(solution)/shard_map/dot_general | solution.py:47
  26.6 4.5 %copy.16 = bf16[1,256,16,256]{3,2,1,0:T(8,128)(2,1)} copy(bf16[1,256,16,256]{1,3,2,0:T(8,128)(2,1)} %get-tuple-element.8) | data formatting | bytes 4194304 | tf_op jit(solution)/shard_map/slice | solution.py:42
  31.1 0.0 copy-start
  31.1 0.0 copy-start.1
  31.1 4.2 %fusion.64 = f32[4096,128]{1,0:T(8,128)} fusion(bf16[4096,256]{1,0:T(8,128)(2,1)} %bitcast.29), kind=kOutput, calls=%fused_computation.96 | convolution fusion | flops 269156352 | bytes 4194304 | tf_op jit(solution)/shard_map/dot_general | solution.py:44
  35.4 0.0 copy-done
  35.4 0.0 copy-done.1
  35.4 1.2 fusion.1
  36.6 1.3 stack.10
  37.9 2.8 %fusion = bf16[4096,128]{1,0:T(8,128)(2,1)S(1)} fusion(f32[4096,128]{1,0:T(8,128)} %fusion.64, bf16[4096,256]{1,0:T(8,128)(2,1)S(1)} %bitcast.28), kind=kOutput, calls=%fused_computation.4 | convolution fusion | flops 270204928 | bytes 5242880 | tf_op jit(solution)/shard_map/dot_general | solution.py:44
  40.7 0.0 copy-start.2
  40.7 0.5 stack.9
  41.2 0.0 copy-start.3
  41.2 0.1 constant_dynamic-update-slice_fusion.1
  41.3 0.6 copy-done.2
  41.9 0.1 constant_dynamic-update-slice_fusion
  42.0 1.5 collective-permute-start.1
  43.5 0.0 copy-done.3
  43.5 7.9 %collective-permute-done.1 = bf16[2,256,256]{2,1,0:T(8,128)(2,1)S(1)} collective-permute-done((bf16[2,256,256]{2,1,0:T(8,128)(2,1)S(1)}, bf16[2,256,256]{2,1,0:T(8,128)(2,1)S(1)}, u32[]{:S(2)}, u32[]{:S(2)}) %collective-permute-start.1) | collective-permute-done | bytes 262176 | tf_op jit(solution)/shard_map/ppermute | solution.py:17
  51.4 0.2 maximum_bitcast_fusion
  51.6 60.6 %copy.18 = bf16[2,32,8,2304]{2,0,1,3:T(2,128)(2,1)} copy(bf16[2,32,8,2304]{3,2,1,0:T(8,128)(2,1)S(1)} %maximum_bitcast_fusion) | data formatting | bytes 4718592 | tf_op jit(solution)/shard_map/reshape | solution.py:93
  112.2 11.5 %gather_fusion.1 = bf16[32,8,2,256]{1,2,3,0:T(2,128)(2,1)} fusion(bf16[32,8,2,2304]{1,2,0,3:T(2,128)(2,1)} %bitcast.26, s32[32]{0:T(128)S(1)} %fusion.72), kind=kCustom, calls=%fused_computation.1 | custom fusion | bytes 524800 | tf_op jit(solution)/shard_map/vmap()/gather | solution.py:97
  123.8 0.0 copy-start.4
  123.8 9.2 %copy.19 = bf16[32,8,2,256]{3,1,2,0:T(8,128)(2,1)} copy(bf16[32,8,2,256]{1,2,3,0:T(2,128)(2,1)} %gather_fusion.1) | data formatting | bytes 524288 | tf_op jit(solution)/shard_map/vmap()/gather | solution.py:97
  133.0 0.0 all-gather.2.cloned.1.call-update
  133.0 0.0 copy-done.4
  133.0 0.1 iota_add_fusion
  133.1 0.1 add.195
  133.2 0.1 broadcast_in_dim.34
  133.3 0.1 broadcast_in_dim.35
  133.4 27.7 %all-gather.2.cloned.1.call-done = bf16[256,8,2,256]{3,1,2,0:T(8,128)(2,1)} async-done(((bf16[32,8,2,256]{3,1,2,0:T(8,128)(2,1)}), bf16[256,8,2,256]{3,1,2,0:T(8,128)(2,1)}) %all-gather.2.cloned.1.call-update) | async-done | bytes 2097168 | tf_op jit(solution)/shard_map/all_gather | solution.py:112
  161.1 2.1 %gather_fusion = bf16[8,8,2,256]{3,1,2,0:T(8,128)(2,1)S(1)} fusion(bf16[256,8,2,256]{3,1,2,0:T(8,128)(2,1)} %all-gather.2.cloned.1.call-done, s32[1024]{0:T(1024)S(1)} %pad_clamp_fusion), kind=kCustom, calls=%fused_computation | custom fusion | bytes 131104 | tf_op jit(solution)/shard_map/jit(_take)/gather | solution.py:113
  163.3 1.4 fusion.48
  164.7 1.4 fusion.49
  166.1 0.5 fusion.14
  166.6 7.6 %convert_bitcast_fusion = bf16[1,1,1024,2048]{3,2,1,0:T(8,128)(2,1)} fusion(bf16[256,1024]{1,0:T(8,128)(2,1)S(1)} %get-tuple-element.6, bf16[256,1024]{1,0:T(8,128)(2,1)S(1)} %get-tuple-element.5, f32[1024]{0:T(1024)S(1)} %multiply_add_fusion.1), kind=kOutput, calls=%fused_computation.8 | convolution fusion | flops 1088421888 | bytes 5246976 | tf_op jit(solution)/shard_map/dot_general | solution.py:86
  (9 shorter events, 0.1 us)
Async XLA Ops:
  6.5 154.6 %all-gather.2.cloned.1.call-start = ((), (), s32[]{:S(2)}) async-start(), calls=%async_computation | async-start | bytes 2359296 | tf_op jit(solution)/shard_map/all_gather | solution.py:112
  9.4 8.4 %collective-permute-start = (bf16[2,256,128]{1,2,0:T(8,128)(2,1)S(1)}, bf16[2,256,128]{1,2,0:T(8,128)(2,1)S(1)}, u32[]{:S(2)}, u32[]{:S(2)}) collective-permute-start(bf16[2,256,128]{1,2,0:T(8,128)(2,1)S(1)} %slice.51), channel_id=1, source_target_pairs={{8,0},{16,8},{24,16},{9,1},{17,9},{25,17},{10,2},{18,10},{26,18},{... | collective-permute-start | bytes 393224 | tf_op jit(solution)/shard_map/ppermute | solution.py:17
  31.1 4.3 %copy-start = (bf16[1,256,16,256]{3,2,1,0:T(8,128)(2,1)S(1)}, bf16[1,256,16,256]{3,2,1,0:T(8,128)(2,1)}, u32[]{:S(2)}) copy-start(bf16[1,256,16,256]{3,2,1,0:T(8,128)(2,1)} %copy.16) | copy-start | bytes 6291460
  31.1 4.3 %copy-start.1 = (f32[4096,128]{1,0:T(8,128)S(1)}, f32[4096,128]{1,0:T(8,128)}, u32[]{:S(2)}) copy-start(f32[4096,128]{1,0:T(8,128)} %fusion.63) | copy-start | bytes 6291460
  40.7 1.2 copy-start.2
  41.2 2.3 %copy-start.3 = (s32[1,32]{1,0:T(1,128)S(1)}, s32[1,32]{1,0:T(1,128)}, u32[]{:S(2)}) copy-start(s32[1,32]{1,0:T(1,128)} %param.5) | copy-start | bytes 388
  42.0 9.4 %collective-permute-start.1 = (bf16[2,256,256]{2,1,0:T(8,128)(2,1)S(1)}, bf16[2,256,256]{2,1,0:T(8,128)(2,1)S(1)}, u32[]{:S(2)}, u32[]{:S(2)}) collective-permute-start(bf16[2,256,256]{2,1,0:T(8,128)(2,1)S(1)} %slice.56), channel_id=1, source_target_pairs={{8,0},{16,8},{24,16},{9,1},{17,9},{25,17},{10,2},{18,10},{26,18},{... | collective-permute-start | bytes 786440 | tf_op jit(solution)/shard_map/ppermute | solution.py:17
  123.8 9.2 %copy-start.4 = (s32[1,1,8]{2,1,0:T(1,128)S(1)}, s32[1,1,8]{2,1,0:T(1,128)}, u32[]{:S(2)}) copy-start(s32[1,1,8]{2,1,0:T(1,128)} %param.4) | copy-start | bytes 100
Sparse Core Ops, SparseCore 0:
  133.1 27.9 all-gather.1
where the time goes:
time: 182 us; the launch traced here: 181 us
  local copies, waits for them, and re-layouts  97.6 us (54%)
  waiting for transfers between devices  42.7 us (23%)
  matrix products  21.3 us (12%)
  between operations  13.6 us (7%)
  other arithmetic  3.22 us (2%)
  starting transfers between devices  2.77 us (2%)
    reshape x1, local copies, waits for them, and re-layouts, cut_windows(): extended.reshape(2, pulses // per_block, per_block, span_bins)  60.6 us
    all_gather x1, waiting for transfers between devices, local(): all_blocks = lax.all_gather(windows, 'tile', axis=0, tiled=True)  27.7 us
    gather x2, local copies, waits for them, and re-layouts, one_block(): return lax.dynamic_slice_in_dim(block_data, start, WIN, 2)  20.7 us
    ppermute x2, waiting for transfers between devices, passed_along(): return lax.ppermute(value, axis, pairs)  15 us
    dot_general x1, matrix products, tile_image(): jnp.dot(interp, focused, preferred_element_type=jnp.float32)  7.65 us
    slice x1, local copies, waits for them, and re-layouts, compress(): real_in = paired[0]  4.49 us
    dot_general x1, matrix products, compress(): jnp.dot(real_in, real_tab, preferred_element_type=jnp.float32)  4.25 us
  transfers between devices with their start and end apart: 3, of which 3 were waited for; matrix products, arithmetic and copies ran while one was open for 0% of the time, Pallas kernels for 0%

commit v1 on v0

--- a/solution.py
+++ b/solution.py
@@ -109,7 +109,24 @@
     my_list = footprint[0, 0]
     tile_pos = lax.axis_index("tile")
     row_pos = lax.axis_index("section")
-    all_blocks = lax.all_gather(windows, "tile", axis=0, tiled=True)
+    length_2, place, rows = (lax.axis_size("tile"), lax.axis_index("tile"), windows.shape[0])
+    ahead = [(i_2, (i_2 + 1) % length_2) for i_2 in range(length_2)]
+    downward = [(i_2, (i_2 - 1) % length_2) for i_2 in range(length_2)]
+    out = jnp.zeros((*windows.shape[:0], length_2 * rows, *windows.shape[0 + 1 :]), windows.dtype)
+    out = lax.dynamic_update_slice_in_dim(out, windows, place * rows, axis=0)
+    from_left = from_right = windows
+    halfway = length_2 // 2
+    for step in range(1, halfway + 1):
+        from_left = lax.ppermute(from_left, "tile", ahead)
+        out = lax.dynamic_update_slice_in_dim(
+            out, from_left, (place - step) % length_2 * rows, axis=0
+        )
+        if step < length_2 - halfway:
+            from_right = lax.ppermute(from_right, "tile", downward)
+            out = lax.dynamic_update_slice_in_dim(
+                out, from_right, (place + step) % length_2 * rows, axis=0
+            )
+    all_blocks = out
     chosen = jnp.take(all_blocks, my_list, axis=0)
     interp = interp_table(PR, WIN)
     image = tile_image(chosen, my_list, row_pos, tile_pos, interp, PC)

time: 182 us -> 169 us (0.929)
  between operations: 13.6 us -> 0.42 us
  starting transfers between devices: 2.77 us -> 10.5 us
  waiting for transfers between devices: 42.7 us -> 38.2 us
  local copies, waits for them, and re-layouts: 97.6 us -> 95.3 us
    all_gather x1 -> x0, waiting for transfers between devices: 27.7 us -> none  [local(): all_blocks = lax.all_gather(windows, 'tile', axis=0, tiled=True)]
    ppermute x0 -> x7, waiting for transfers between devices: none -> 23.1 us  [the longest x4 23.1 us: local(): from_left = lax.ppermute(from_left, 'tile', ahead)]
    ppermute x0 -> x7, starting transfers between devices: none -> 7.95 us  [the longest x3 7.88 us: local(): from_right = lax.ppermute(from_right, 'tile', downward)]
  transfers between devices with their start and end apart: 3 -> 9, of which waited for: 3 -> 6; matrix products, arithmetic and copies ran while one was open for 0% -> 0% of each run, Pallas kernels for 0% -> 0%
where the time goes in v1:
time: 169 us
  local copies, waits for them, and re-layouts  95.3 us (56%)
  waiting for transfers between devices  38.2 us (23%)
  matrix products  21.2 us (13%)
  starting transfers between devices  10.5 us (6%)
  other arithmetic  3.23 us (2%)
    reshape x1, local copies, waits for them, and re-layouts, cut_windows(): extended.reshape(2, pulses // per_block, per_block, span_bins)  60.7 us
    ppermute x4, waiting for transfers between devices, local(): from_left = lax.ppermute(from_left, 'tile', ahead)  23.1 us
    gather x2, local copies, waits for them, and re-layouts, one_block(): return lax.dynamic_slice_in_dim(block_data, start, WIN, 2)  19.7 us
    ppermute x2, waiting for transfers between devices, passed_along(): return lax.ppermute(value, axis, pairs)  15.1 us
    ppermute x3, starting transfers between devices, local(): from_right = lax.ppermute(from_right, 'tile', downward)  7.88 us
    dot_general x1, matrix products, tile_image(): jnp.dot(interp, focused, preferred_element_type=jnp.float32)  7.65 us
    slice x1, local copies, waits for them, and re-layouts, compress(): real_in = paired[0]  4.49 us
    dot_general x1, matrix products, compress(): jnp.dot(real_in, real_tab, preferred_element_type=jnp.float32)  4.26 us
  transfers between devices with their start and end apart: 9, of which 6 were waited for; matrix products, arithmetic and copies ran while one was open for 0% of the time, Pallas kernels for 0%

profile of v1, /device:TPU:0, one launch (start us, length us, event | category | flops | bytes accessed | tf_op | source)
XLA Modules:
  0.0 168.9 jit_solution(7943359819171000134)
XLA Ops:
  0.0 2.9 %copy.21 = bf16[2,256,2048]{1,2,0:T(8,128)(2,1)S(1)} copy(bf16[2,256,2048]{2,1,0:T(8,128)(2,1)} %param.3) | data formatting | bytes 4194304 | tf_op args[0]
  2.9 1.3 collective-permute-start
  4.2 7.1 %collective-permute-done = bf16[2,256,128]{1,2,0:T(8,128)(2,1)S(1)} collective-permute-done((bf16[2,256,128]{1,2,0:T(8,128)(2,1)S(1)}, bf16[2,256,128]{1,2,0:T(8,128)(2,1)S(1)}, u32[]{:S(2)}, u32[]{:S(2)}) %collective-permute-start) | collective-permute-done | bytes 131104 | tf_op jit(solution)/shard_map/ppermute | solution.py:17
  11.3 0.1 pad_maximum_fusion
  11.5 0.5 fusion.123
  12.0 2.3 %pad_maximum_fusion.1 = (bf16[1,256,16,256]{1,3,2,0:T(8,128)(2,1)}, bf16[1,256,16,256]{1,3,2,0:T(8,128)(2,1)}) fusion(bf16[2,256,16,128]{1,3,2,0:T(8,128)(2,1)S(1)} %get-tuple-element.9, bf16[2,256,16,128]{1,3,2,0:T(8,128)(2,1)S(1)} %get-tuple-element.10), kind=kLoop, calls=%fused_computation.12 | loop fusion | flops 8388608 | bytes 8388608 | tf_op jit(solution)/shard_map/concatenate | solution.py:39
  14.2 3.3 %copy.23 = bf16[1,256,16,256]{3,2,1,0:T(8,128)(2,1)S(1)} copy(bf16[1,256,16,256]{1,3,2,0:T(8,128)(2,1)} %get-tuple-element.7) | data formatting | bytes 4194304 | tf_op jit(solution)/shard_map/slice | solution.py:43
  17.6 2.5 %fusion.63 = f32[4096,128]{1,0:T(8,128)} fusion(bf16[4096,256]{1,0:T(8,128)(2,1)S(1)} %bitcast.27), kind=kOutput, calls=%fused_computation.95 | convolution fusion | flops 269156352 | bytes 4194304 | tf_op jit(solution)/shard_map/dot_general | solution.py:47
  20.1 4.5 %copy.22 = bf16[1,256,16,256]{3,2,1,0:T(8,128)(2,1)} copy(bf16[1,256,16,256]{1,3,2,0:T(8,128)(2,1)} %get-tuple-element.8) | data formatting | bytes 4194304 | tf_op jit(solution)/shard_map/slice | solution.py:42
  24.6 4.3 %fusion.64 = f32[4096,128]{1,0:T(8,128)} fusion(bf16[4096,256]{1,0:T(8,128)(2,1)} %bitcast.29), kind=kOutput, calls=%fused_computation.96 | convolution fusion | flops 269156352 | bytes 4194304 | tf_op jit(solution)/shard_map/dot_general | solution.py:44
  28.9 1.2 fusion.1
  30.1 1.3 stack.10
  31.4 2.8 %fusion = bf16[4096,128]{1,0:T(8,128)(2,1)S(1)} fusion(f32[4096,128]{1,0:T(8,128)} %fusion.64, bf16[4096,256]{1,0:T(8,128)(2,1)S(1)} %bitcast.28), kind=kOutput, calls=%fused_computation.4 | convolution fusion | flops 270204928 | bytes 5242880 | tf_op jit(solution)/shard_map/dot_general | solution.py:44
  34.2 0.0 copy-start.2
  34.2 0.5 stack.9
  34.7 0.0 copy-start.3
  34.7 0.1 constant_dynamic-update-slice_fusion.1
  34.8 0.6 copy-done.2
  35.4 0.1 constant_dynamic-update-slice_fusion
  35.5 1.3 collective-permute-start.1
  36.8 0.1 iota_add_fusion
  36.9 8.0 %collective-permute-done.1 = bf16[2,256,256]{2,1,0:T(8,128)(2,1)S(1)} collective-permute-done((bf16[2,256,256]{2,1,0:T(8,128)(2,1)S(1)}, bf16[2,256,256]{2,1,0:T(8,128)(2,1)S(1)}, u32[]{:S(2)}, u32[]{:S(2)}) %collective-permute-start.1) | collective-permute-done | bytes 262176 | tf_op jit(solution)/shard_map/ppermute | solution.py:17
  44.9 0.2 maximum_bitcast_fusion
  45.1 60.7 %copy.24 = bf16[2,32,8,2304]{2,0,1,3:T(2,128)(2,1)} copy(bf16[2,32,8,2304]{3,2,1,0:T(8,128)(2,1)S(1)} %maximum_bitcast_fusion) | data formatting | bytes 4718592 | tf_op jit(solution)/shard_map/reshape | solution.py:93
  105.8 11.5 %gather_fusion.1 = bf16[32,8,2,256]{1,2,3,0:T(2,128)(2,1)} fusion(bf16[32,8,2,2304]{1,2,0,3:T(2,128)(2,1)} %bitcast.26, s32[32]{0:T(128)S(1)} %fusion.78), kind=kCustom, calls=%fused_computation.1 | custom fusion | bytes 524800 | tf_op jit(solution)/shard_map/vmap()/gather | solution.py:97
  117.3 8.1 %copy.25 = bf16[32,8,2,256]{3,1,2,0:T(8,128)(2,1)S(1)} copy(bf16[32,8,2,256]{1,2,3,0:T(2,128)(2,1)} %gather_fusion.1) | data formatting | bytes 524288 | tf_op jit(solution)/shard_map/vmap()/gather | solution.py:97
  125.5 0.1 collective-permute-start.2
  125.6 2.6 %collective-permute-start.3 = (bf16[32,8,2,256]{3,1,2,0:T(8,128)(2,1)S(1)}, bf16[32,8,2,256]{3,1,2,0:T(8,128)(2,1)S(1)}, u32[]{:S(2)}, u32[]{:S(2)}) collective-permute-start(bf16[32,8,2,256]{3,1,2,0:T(8,128)(2,1)S(1)} %copy.25), channel_id=1, source_target_pairs={{0,7},{1,0},{2,1},{3,2},{4,3},{5,4},{6,5},{7,6},{8,15},{9,8},{10,9... | collective-permute-start | bytes 786440 | tf_op jit(solution)/shard_map/ppermute | solution.py:125
  128.2 5.1 %collective-permute-done.2 = bf16[32,8,2,256]{3,1,2,0:T(8,128)(2,1)S(1)} collective-permute-done((bf16[32,8,2,256]{3,1,2,0:T(8,128)(2,1)S(1)}, bf16[32,8,2,256]{3,1,2,0:T(8,128)(2,1)S(1)}, u32[]{:S(2)}, u32[]{:S(2)}) %collective-permute-start.2) | collective-permute-done | bytes 262176 | tf_op jit(solution)/shard_map/ppermute | solution.py:120
  133.3 0.0 collective-permute-start.4
  133.4 0.1 add.272
  133.5 0.1 broadcast_in_dim.37
  133.6 0.1 broadcast_in_dim.38
  133.7 2.6 %collective-permute-start.5 = (bf16[32,8,2,256]{3,1,2,0:T(8,128)(2,1)S(1)}, bf16[32,8,2,256]{3,1,2,0:T(8,128)(2,1)S(1)}, u32[]{:S(2)}, u32[]{:S(2)}) collective-permute-start(bf16[32,8,2,256]{3,1,2,0:T(8,128)(2,1)S(1)} %collective-permute-done.3), channel_id=1, source_target_pairs={{0,7},{1,0},{2,1},{3,2},{4,3},{5,4},{6,5},{7,6},{8,15},{9,8},{10,9... | collective-permute-start | bytes 786440 | tf_op jit(solution)/shard_map/ppermute | solution.py:125
  136.3 0.1 broadcast_in_dim.40
  136.4 5.2 %collective-permute-done.4 = bf16[32,8,2,256]{3,1,2,0:T(8,128)(2,1)S(1)} collective-permute-done((bf16[32,8,2,256]{3,1,2,0:T(8,128)(2,1)S(1)}, bf16[32,8,2,256]{3,1,2,0:T(8,128)(2,1)S(1)}, u32[]{:S(2)}, u32[]{:S(2)}) %collective-permute-start.4) | collective-permute-done | bytes 262176 | tf_op jit(solution)/shard_map/ppermute | solution.py:120
  141.6 0.0 collective-permute-start.6
  141.7 0.0 collective-permute-done.5
  141.7 2.7 %collective-permute-start.7 = (bf16[32,8,2,256]{3,1,2,0:T(8,128)(2,1)S(1)}, bf16[32,8,2,256]{3,1,2,0:T(8,128)(2,1)S(1)}, u32[]{:S(2)}, u32[]{:S(2)}) collective-permute-start(bf16[32,8,2,256]{3,1,2,0:T(8,128)(2,1)S(1)} %collective-permute-done.5), channel_id=1, source_target_pairs={{0,7},{1,0},{2,1},{3,2},{4,3},{5,4},{6,5},{7,6},{8,15},{9,8},{10,9... | collective-permute-start | bytes 786440 | tf_op jit(solution)/shard_map/ppermute | solution.py:125
  144.4 6.2 %collective-permute-done.6 = bf16[32,8,2,256]{3,1,2,0:T(8,128)(2,1)S(1)} collective-permute-done((bf16[32,8,2,256]{3,1,2,0:T(8,128)(2,1)S(1)}, bf16[32,8,2,256]{3,1,2,0:T(8,128)(2,1)S(1)}, u32[]{:S(2)}, u32[]{:S(2)}) %collective-permute-start.6) | collective-permute-done | bytes 262176 | tf_op jit(solution)/shard_map/ppermute | solution.py:120
  150.7 0.0 collective-permute-start.8
  150.7 0.0 collective-permute-done.7
  150.8 6.6 %collective-permute-done.8 = bf16[32,8,2,256]{3,1,2,0:T(8,128)(2,1)S(1)} collective-permute-done((bf16[32,8,2,256]{3,1,2,0:T(8,128)(2,1)S(1)}, bf16[32,8,2,256]{3,1,2,0:T(8,128)(2,1)S(1)}, u32[]{:S(2)}, u32[]{:S(2)}) %collective-permute-start.8) | collective-permute-done | bytes 262176 | tf_op jit(solution)/shard_map/ppermute | solution.py:120
  157.4 0.6 gather_fusion
  157.9 1.4 fusion.48
  159.3 1.4 fusion.49
  160.8 0.5 fusion.14
  161.3 7.6 %convert_bitcast_fusion = bf16[1,1,1024,2048]{3,2,1,0:T(8,128)(2,1)} fusion(bf16[256,1024]{1,0:T(8,128)(2,1)S(1)} %get-tuple-element.6, bf16[256,1024]{1,0:T(8,128)(2,1)S(1)} %get-tuple-element.5, f32[1024]{0:T(1024)S(1)} %multiply_add_fusion.1), kind=kOutput, calls=%fused_computation.8 | convolution fusion | flops 1088421888 | bytes 5246976 | tf_op jit(solution)/shard_map/dot_general | solution.py:86
  (25 shorter events, 0.3 us)
Async XLA Ops:
  0.0 4.2 %copy-start.4 = (s32[1,1,8]{2,1,0:T(1,128)S(1)}, s32[1,1,8]{2,1,0:T(1,128)}, u32[]{:S(2)}) copy-start(s32[1,1,8]{2,1,0:T(1,128)} %param.4) | copy-start | bytes 100
  2.9 8.4 %collective-permute-start = (bf16[2,256,128]{1,2,0:T(8,128)(2,1)S(1)}, bf16[2,256,128]{1,2,0:T(8,128)(2,1)S(1)}, u32[]{:S(2)}, u32[]{:S(2)}) collective-permute-start(bf16[2,256,128]{1,2,0:T(8,128)(2,1)S(1)} %slice.51), channel_id=1, source_target_pairs={{8,0},{16,8},{24,16},{9,1},{17,9},{25,17},{10,2},{18,10},{26,18},{... | collective-permute-start | bytes 393224 | tf_op jit(solution)/shard_map/ppermute | solution.py:17
  24.6 4.3 %copy-start = (bf16[1,256,16,256]{3,2,1,0:T(8,128)(2,1)S(1)}, bf16[1,256,16,256]{3,2,1,0:T(8,128)(2,1)}, u32[]{:S(2)}) copy-start(bf16[1,256,16,256]{3,2,1,0:T(8,128)(2,1)} %copy.22) | copy-start | bytes 6291460
  24.6 4.3 %copy-start.1 = (f32[4096,128]{1,0:T(8,128)S(1)}, f32[4096,128]{1,0:T(8,128)}, u32[]{:S(2)}) copy-start(f32[4096,128]{1,0:T(8,128)} %fusion.63) | copy-start | bytes 6291460
  34.2 1.2 copy-start.2
  34.7 2.1 %copy-start.3 = (s32[1,32]{1,0:T(1,128)S(1)}, s32[1,32]{1,0:T(1,128)}, u32[]{:S(2)}) copy-start(s32[1,32]{1,0:T(1,128)} %param.5) | copy-start | bytes 388
  35.5 9.4 %collective-permute-start.1 = (bf16[2,256,256]{2,1,0:T(8,128)(2,1)S(1)}, bf16[2,256,256]{2,1,0:T(8,128)(2,1)S(1)}, u32[]{:S(2)}, u32[]{:S(2)}) collective-permute-start(bf16[2,256,256]{2,1,0:T(8,128)(2,1)S(1)} %slice.56), channel_id=1, source_target_pairs={{8,0},{16,8},{24,16},{9,1},{17,9},{25,17},{10,2},{18,10},{26,18},{... | collective-permute-start | bytes 786440 | tf_op jit(solution)/shard_map/ppermute | solution.py:17
  125.5 7.8 %collective-permute-start.2 = (bf16[32,8,2,256]{3,1,2,0:T(8,128)(2,1)S(1)}, bf16[32,8,2,256]{3,1,2,0:T(8,128)(2,1)S(1)}, u32[]{:S(2)}, u32[]{:S(2)}) collective-permute-start(bf16[32,8,2,256]{3,1,2,0:T(8,128)(2,1)S(1)} %copy.25), channel_id=1, source_target_pairs={{0,1},{1,2},{2,3},{3,4},{4,5},{5,6},{6,7},{7,0},{8,9},{9,10},{10,1... | collective-permute-start | bytes 786440 | tf_op jit(solution)/shard_map/ppermute | solution.py:120
  125.6 8.1 %collective-permute-start.3 = (bf16[32,8,2,256]{3,1,2,0:T(8,128)(2,1)S(1)}, bf16[32,8,2,256]{3,1,2,0:T(8,128)(2,1)S(1)}, u32[]{:S(2)}, u32[]{:S(2)}) collective-permute-start(bf16[32,8,2,256]{3,1,2,0:T(8,128)(2,1)S(1)} %copy.25), channel_id=1, source_target_pairs={{0,7},{1,0},{2,1},{3,2},{4,3},{5,4},{6,5},{7,6},{8,15},{9,8},{10,9... | collective-permute-start | bytes 786440 | tf_op jit(solution)/shard_map/ppermute | solution.py:125
  133.3 8.4 %collective-permute-start.4 = (bf16[32,8,2,256]{3,1,2,0:T(8,128)(2,1)S(1)}, bf16[32,8,2,256]{3,1,2,0:T(8,128)(2,1)S(1)}, u32[]{:S(2)}, u32[]{:S(2)}) collective-permute-start(bf16[32,8,2,256]{3,1,2,0:T(8,128)(2,1)S(1)} %collective-permute-done.2), channel_id=1, source_target_pairs={{0,1},{1,2},{2,3},{3,4},{4,5},{5,6},{6,7},{7,0},{8,9},{9,10},{10,1... | collective-permute-start | bytes 786440 | tf_op jit(solution)/shard_map/ppermute | solution.py:120
  133.7 8.0 %collective-permute-start.5 = (bf16[32,8,2,256]{3,1,2,0:T(8,128)(2,1)S(1)}, bf16[32,8,2,256]{3,1,2,0:T(8,128)(2,1)S(1)}, u32[]{:S(2)}, u32[]{:S(2)}) collective-permute-start(bf16[32,8,2,256]{3,1,2,0:T(8,128)(2,1)S(1)} %collective-permute-done.3), channel_id=1, source_target_pairs={{0,7},{1,0},{2,1},{3,2},{4,3},{5,4},{6,5},{7,6},{8,15},{9,8},{10,9... | collective-permute-start | bytes 786440 | tf_op jit(solution)/shard_map/ppermute | solution.py:125
  141.6 9.0 %collective-permute-start.6 = (bf16[32,8,2,256]{3,1,2,0:T(8,128)(2,1)S(1)}, bf16[32,8,2,256]{3,1,2,0:T(8,128)(2,1)S(1)}, u32[]{:S(2)}, u32[]{:S(2)}) collective-permute-start(bf16[32,8,2,256]{3,1,2,0:T(8,128)(2,1)S(1)} %collective-permute-done.4), channel_id=1, source_target_pairs={{0,1},{1,2},{2,3},{3,4},{4,5},{5,6},{6,7},{7,0},{8,9},{9,10},{10,1... | collective-permute-start | bytes 786440 | tf_op jit(solution)/shard_map/ppermute | solution.py:120
  141.7 9.0 %collective-permute-start.7 = (bf16[32,8,2,256]{3,1,2,0:T(8,128)(2,1)S(1)}, bf16[32,8,2,256]{3,1,2,0:T(8,128)(2,1)S(1)}, u32[]{:S(2)}, u32[]{:S(2)}) collective-permute-start(bf16[32,8,2,256]{3,1,2,0:T(8,128)(2,1)S(1)} %collective-permute-done.5), channel_id=1, source_target_pairs={{0,7},{1,0},{2,1},{3,2},{4,3},{5,4},{6,5},{7,6},{8,15},{9,8},{10,9... | collective-permute-start | bytes 786440 | tf_op jit(solution)/shard_map/ppermute | solution.py:125
  150.7 6.7 %collective-permute-start.8 = (bf16[32,8,2,256]{3,1,2,0:T(8,128)(2,1)S(1)}, bf16[32,8,2,256]{3,1,2,0:T(8,128)(2,1)S(1)}, u32[]{:S(2)}, u32[]{:S(2)}) collective-permute-start(bf16[32,8,2,256]{3,1,2,0:T(8,128)(2,1)S(1)} %collective-permute-done.6), channel_id=1, source_target_pairs={{0,1},{1,2},{2,3},{3,4},{4,5},{5,6},{6,7},{7,0},{8,9},{9,10},{10,1... | collective-permute-start | bytes 786440 | tf_op jit(solution)/shard_map/ppermute | solution.py:120
